TPU v7x, 32 devices: a whole 2x2x4 slice. The times are simulated.
32 devices in a mesh: row: 4 (over y, x), col: 8 (over z, core).
Axes of the slice: x: 2, y: 2, z: 4, core: 2. Of those that a mesh axis runs over, the one named last changes fastest.
Arguments:
- b_steps: float32 [2, 1024, 2048], P(None, 'row', 'col'), may hold values from -6 to 6
- b_trail: float32 [4096, 2048], P('row', 'col'), may hold values from -6 to 6
- l_cross: float32 [1024, 1024], P('row', 'col'), may hold values from -0.1875 to 0.1875
- l_trail: float32 [2, 4096, 1024], P(None, 'row', 'col'), may hold values from -0.125 to 0.125
- diag_inv: float32 [2, 2, 512, 512], P(None, None, None, 'col'), may hold values from -1.5 to 1.5, as said below
- diag_low: float32 [2, 512, 512], P(None, None, 'col'), may hold values from -0.25 to 0.25
Outputs:
- x_steps: float32 [2, 1024, 2048], P(None, 'row', 'col')
- trail_out: float32 [4096, 2048], P('row', 'col')
Inputs may be any that keep to these rules, and one draw needn't show every extreme that they name: Each diag_inv[s, h] is lower triangular with diagonal entries of 0.5 to 1.5 and strictly lower entries of magnitude at most 3 / sqrt(512).
All inputs are finite; a program needn't handle non-finite values.
Results may differ from a plain program's by a relative error of at most 0.00013.
Values sent between devices are 32-bit elements; how exact they have to be, the bound alone decides.
No kernel may reach another device: no remote copies, remote signals or barrier semaphores. Data moves between devices by JAX's collectives and lax.ppermute only.
A program may use at most 64 MiB of HBM per device.

v0:
```python
import jax
import jax.numpy as jnp
from jax import lax
from jax.sharding import PartitionSpec as P

exact_prec = lax.Precision.HIGHEST


def mult(left_mat, right_mat):
    return jnp.dot(left_mat, right_mat, precision=exact_prec, preferred_element_type=jnp.float32)


def inverse_columns(diag_inv, diag_low, section, offset, own_rows):
    inv_first = diag_inv[section, 0]
    inv_second = diag_inv[section, 1]
    low_block = diag_low[section]
    first_all, second_all, low_all = (
        lax.all_gather(inv_first, "col", axis=1, tiled=True),
        lax.all_gather(inv_second, "col", axis=1, tiled=True),
        lax.all_gather(low_block, "col", axis=1, tiled=True),
    )
    half_rows = first_all.shape[0]
    first_at = jnp.minimum(offset, half_rows - own_rows)
    chosen = lax.dynamic_slice_in_dim(first_all, first_at, own_rows, 1)
    upper = jnp.concatenate([chosen, -mult(second_all, mult(low_all, chosen))], 0)
    second_at = jnp.clip(offset - half_rows, 0, half_rows - own_rows)
    picked = lax.dynamic_slice_in_dim(second_all, second_at, own_rows, 1)
    bottom = jnp.concatenate([jnp.zeros((half_rows, own_rows), jnp.float32), picked], 0)
    return jnp.where(offset < half_rows, upper, bottom)


def solve_step(diag_inv, diag_low, section, offset, own_rows, rows_block):
    inverse_cols = inverse_columns(diag_inv, diag_low, section, offset, own_rows)
    return lax.psum(mult(inverse_cols, rows_block), "row")


def shards(b_steps, b_trail, l_cross, l_trail, diag_inv, diag_low):
    own_rows = b_steps.shape[1]
    offset = lax.axis_index("row") * own_rows
    solved_first = solve_step(diag_inv, diag_low, 0, offset, own_rows, b_steps[0])
    segment = solved_first
    next_rows = b_steps[1] - mult(lax.all_gather(l_cross, "col", axis=1, tiled=True), segment)
    trail = b_trail - mult(lax.all_gather(l_trail[0], "col", axis=1, tiled=True), segment)
    solved_second = solve_step(diag_inv, diag_low, 1, offset, own_rows, next_rows)
    segment = solved_second
    trail = trail - mult(lax.all_gather(l_trail[1], "col", axis=1, tiled=True), segment)
    mine_first = lax.dynamic_slice_in_dim(solved_first, offset, own_rows, 0)
    mine_second = lax.dynamic_slice_in_dim(solved_second, offset, own_rows, 0)
    return (jnp.stack([mine_first, mine_second]), trail)


def solution(mesh):
    placed = (
        P(None, "row", "col"),
        P("row", "col"),
        P("row", "col"),
        P(None, "row", "col"),
        P(None, None, None, "col"),
        P(None, None, "col"),
    )
    return jax.shard_map(
        shards,
        mesh=mesh,
        in_specs=placed,
        out_specs=(P(None, "row", "col"), P("row", "col")),
        check_vma=False,
    )
```

profile of v0, /device:TPU:0, one launch (start us, length us, event | category | flops | bytes accessed | tf_op | source)
XLA Modules:
  0.0 404.8 jit_solution(14901719577600979641)
XLA Ops:
  7.2 1.9 fusion.42
  9.2 0.7 all-gather.24.cloned.1.call-update
  10.0 1.7 fusion.43
  13.5 0.7 all-gather.18.cloned.1.call-update
  14.3 20.3 %all-gather.20.cloned.1.call-done = f32[1,1,512,512]{2,3,1,0:T(8,128)} async-done(((f32[1,1,512,64]{2,3,1,0:T(8,128)}), f32[1,1,512,512]{2,3,1,0:T(8,128)}) %all-gather.20.cloned.1.call-update) | async-done | bytes 1048592 | tf_op jit(solution)/shard_map/all_gather | solution.py:18
  34.6 1.1 dynamic-slice_bitcast_fusion.3
  35.7 22.9 %all-gather.24.cloned.1.call-done = f32[1,1,512,512]{2,3,1,0:T(8,128)} async-done(((f32[1,1,512,64]{2,3,1,0:T(8,128)}), f32[1,1,512,512]{2,3,1,0:T(8,128)}) %all-gather.24.cloned.1.call-update) | async-done | bytes 1048592 | tf_op jit(solution)/shard_map/all_gather | solution.py:19
  58.6 1.1 dynamic-slice_bitcast_fusion.2
  59.7 22.4 %all-gather.22.cloned.1.call-done = f32[1,512,512]{1,2,0:T(8,128)} async-done(((f32[1,512,64]{1,2,0:T(8,128)}), f32[1,512,512]{1,2,0:T(8,128)}) %all-gather.22.cloned.1.call-update) | async-done | bytes 1048592 | tf_op jit(solution)/shard_map/all_gather | solution.py:20
  82.1 2.3 fusion.29
  84.4 2.3 fusion.17
  86.7 2.8 fusion.19
  89.5 15.9 %all-gather.26.cloned.1.call-done = f32[1,1,512,512]{2,3,1,0:T(8,128)} async-done(((f32[1,1,512,64]{2,3,1,0:T(8,128)}), f32[1,1,512,512]{2,3,1,0:T(8,128)}) %all-gather.26.cloned.1.call-update) | async-done | bytes 1048592 | tf_op jit(solution)/shard_map/all_gather | solution.py:18
  105.4 1.1 dynamic-slice_bitcast_fusion.1
  106.6 22.8 %all-gather.30.cloned.1.call-done = f32[1,1,512,512]{2,3,1,0:T(8,128)} async-done(((f32[1,1,512,64]{2,3,1,0:T(8,128)}), f32[1,1,512,512]{2,3,1,0:T(8,128)}) %all-gather.30.cloned.1.call-update) | async-done | bytes 1048592 | tf_op jit(solution)/shard_map/all_gather | solution.py:19
  129.3 1.1 dynamic-slice_bitcast_fusion
  130.5 22.2 %all-gather.28.cloned.1.call-done = f32[1,512,512]{1,2,0:T(8,128)} async-done(((f32[1,512,64]{1,2,0:T(8,128)}), f32[1,512,512]{1,2,0:T(8,128)}) %all-gather.28.cloned.1.call-update) | async-done | bytes 1048592 | tf_op jit(solution)/shard_map/all_gather | solution.py:20
  152.7 2.3 fusion.26
  155.0 2.3 fusion.16
  157.2 20.6 %all-gather.18.cloned.1.call-done = f32[256,1024]{1,0:T(8,128)} async-done(((f32[256,128]{1,0:T(8,128)}), f32[256,1024]{1,0:T(8,128)}) %all-gather.18.cloned.1.call-update) | async-done | bytes 1048592 | tf_op jit(solution)/shard_map/all_gather | solution.py:42
  177.8 54.9 %all-reduce.5.cloned.1.call-done = f32[1024,256]{1,0:T(8,128)} async-done(((f32[1024,256]{1,0:T(8,128)}), f32[1024,256]{1,0:T(8,128)}) %all-reduce.5.cloned.1.call-update) | async-done | bytes 1048592 | tf_op jit(solution)/shard_map/psum | solution.py:34
  232.7 2.6 fusion.18
  235.3 2.8 fusion.22
  238.1 2.3 fusion.41
  241.6 49.1 %all-reduce.7.cloned.1.call-done = f32[1024,256]{1,0:T(8,128)} async-done(((f32[1024,256]{1,0:T(8,128)}), f32[1024,256]{1,0:T(8,128)}) %all-reduce.7.cloned.1.call-update) | async-done | bytes 1048592 | tf_op jit(solution)/shard_map/psum | solution.py:34
  290.7 1.0 dynamic-slice_bitcast_fusion.4
  291.7 0.8 pad_maximum_fusion
  292.5 47.5 %all-gather.34.cloned.1.call-done = f32[1,1024,1024]{2,1,0:T(8,128)} async-done(((f32[1,1024,128]{2,1,0:T(8,128)}), f32[1,1024,1024]{2,1,0:T(8,128)}) %all-gather.34.cloned.1.call-update) | async-done | bytes 4194320 | tf_op jit(solution)/shard_map/all_gather | solution.py:46
  340.0 10.3 %fusion.13 = f32[1024,256]{0,1:T(8,128)} fusion(f32[1024,256]{1,0:T(8,128)} %all-reduce.7.cloned.1.call-done, f32[1,1024,1024]{2,1,0:T(8,128)} %all-gather.34.cloned.1.call-done), kind=kOutput, calls=%fused_computation.7 | convolution fusion | flops 3221225472 | bytes 6291456 | tf_op jit(solution)/shard_map/dot_general | solution.py:10
  350.3 37.3 %all-gather.32.cloned.1.call-done = f32[1,1024,1024]{2,1,0:T(8,128)} async-done(((f32[1,1024,128]{2,1,0:T(8,128)}), f32[1,1024,1024]{2,1,0:T(8,128)}) %all-gather.32.cloned.1.call-update) | async-done | bytes 4194320 | tf_op jit(solution)/shard_map/all_gather | solution.py:43
  387.6 9.3 %fusion.10 = f32[1024,256]{0,1:T(8,128)S(1)} fusion(f32[1024,256]{0,1:T(8,128)} %fusion.13, f32[1024,256]{0,1:T(8,128)S(1)} %copy.8, f32[1024,256]{1,0:T(8,128)S(1)} %copy-done, f32[1,1024,1024]{2,1,0:T(8,128)} %all-gather.32.cloned.1.call-done), kind=kOutput, calls=%fused_computation.6 | convolution fusion | flops 3221749760 | bytes 8388608 | tf_op jit(solution)/shard_map/dot_general | solution.py:10
  396.9 1.3 copy.9
  (28 shorter events, 3.1 us)
Async XLA Ops:
  7.2 79.5 %copy-start.2 = (f32[2,256,256]{2,1,0:T(8,128)S(1)}, f32[2,256,256]{2,1,0:T(8,128)}, u32[]{:S(2)}) copy-start(f32[2,256,256]{2,1,0:T(8,128)} %param.6) | copy-start | bytes 1572868
  7.2 27.4 %all-gather.20.cloned.1.call-start = ((), (), s32[]{:S(2)}) async-start(), calls=%async_computation.3 | async-start | bytes 1179648 | tf_op jit(solution)/shard_map/all_gather | solution.py:18
  9.2 49.5 %all-gather.24.cloned.1.call-start = ((), (), s32[]{:S(2)}) async-start(), calls=%async_computation.5 | async-start | bytes 1179648 | tf_op jit(solution)/shard_map/all_gather | solution.py:19
  9.9 72.2 %all-gather.22.cloned.1.call-start = ((), (), s32[]{:S(2)}) async-start(), calls=%async_computation.4 | async-start | bytes 1179648 | tf_op jit(solution)/shard_map/all_gather | solution.py:20
  11.7 93.7 %all-gather.26.cloned.1.call-start = ((), (), s32[]{:S(2)}) async-start(), calls=%async_computation.6 | async-start | bytes 1179648 | tf_op jit(solution)/shard_map/all_gather | solution.py:18
  12.3 117.0 %all-gather.30.cloned.1.call-start = ((), (), s32[]{:S(2)}) async-start(), calls=%async_computation.8 | async-start | bytes 1179648 | tf_op jit(solution)/shard_map/all_gather | solution.py:19
  12.9 139.8 %all-gather.28.cloned.1.call-start = ((), (), s32[]{:S(2)}) async-start(), calls=%async_computation.7 | async-start | bytes 1179648 | tf_op jit(solution)/shard_map/all_gather | solution.py:20
  13.5 164.3 %all-gather.18.cloned.1.call-start = ((), (), s32[]{:S(2)}) async-start(), calls=%async_computation.1 | async-start | bytes 1179648 | tf_op jit(solution)/shard_map/all_gather | solution.py:42
  14.2 218.5 %all-reduce.5.cloned.1.call-start = ((), (), s32[]{:S(2)}) async-start(), calls=%async_computation | async-start | bytes 2097152 | tf_op jit(solution)/shard_map/psum | solution.py:34
  89.5 201.2 %all-reduce.7.cloned.1.call-start = ((), (), s32[]{:S(2)}) async-start(), calls=%async_computation.2 | async-start | bytes 2097152 | tf_op jit(solution)/shard_map/psum | solution.py:34
  235.3 6.3 %copy-start = (f32[1024,256]{1,0:T(8,128)S(1)}, f32[1024,256]{1,0:T(8,128)}, u32[]{:S(2)}) copy-start(f32[1024,256]{1,0:T(8,128)} %all-reduce.5.cloned.1.call-done) | copy-start | bytes 3145732
  238.1 3.2 copy-start.1
  238.1 101.9 %all-gather.34.cloned.1.call-start = ((), (), s32[]{:S(2)}) async-start(), calls=%async_computation.10 | async-start | bytes 4718592 | tf_op jit(solution)/shard_map/all_gather | solution.py:46
  240.5 147.1 %all-gather.32.cloned.1.call-start = ((), (), s32[]{:S(2)}) async-start(), calls=%async_computation.9 | async-start | bytes 4718592 | tf_op jit(solution)/shard_map/all_gather | solution.py:43
Sparse Core Ops, SparseCore 0:
  9.6 24.9 all-gather.19
  36.7 21.8 all-gather.23
  60.2 21.8 all-gather.21
  83.6 21.8 all-gather.25
  107.5 21.8 all-gather.29
  130.8 21.8 all-gather.27
  154.3 23.4 all-gather.17
  181.4 51.1 all-reduce.4
  238.2 52.4 all-reduce.6
  292.2 47.8 all-gather.33
  341.6 45.9 all-gather.31
where the time goes:
time: 405 us
  waiting for transfers between devices  339 us (84%)
  matrix products  36.8 us (9%)
  between operations  14 us (3%)
  local copies, waits for them, and re-layouts  13 us (3%)
    psum x2, waiting for transfers between devices, solve_step(): return lax.psum(mult(inverse_cols, rows_block), 'row')  104 us
    all_gather x1, waiting for transfers between devices, shards(): lax.all_gather(l_trail[1], 'col', axis=1, tiled=True)  47.5 us
    all_gather x2, waiting for transfers between devices, inverse_columns(): lax.all_gather(inv_second, 'col', axis=1, tiled=True)  45.7 us
    all_gather x2, waiting for transfers between devices, inverse_columns(): lax.all_gather(low_block, 'col', axis=1, tiled=True)  44.6 us
    all_gather x1, waiting for transfers between devices, shards(): lax.all_gather(l_trail[0], 'col', axis=1, tiled=True)  37.3 us
    dot_general x9, matrix products, mult(): jnp.dot(left_mat, right_mat, precision=exact_prec, preferred_element_type...  36.8 us
    all_gather x2, waiting for transfers between devices, inverse_columns(): lax.all_gather(inv_first, 'col', axis=1, tiled=True)  36.2 us
    all_gather x1, waiting for transfers between devices, shards(): lax.all_gather(l_cross, 'col', axis=1, tiled=True)  20.6 us
  transfers between devices with their start and end apart: 11, of which 11 were waited for; matrix products, arithmetic and copies ran while one was open for 8% of the time, Pallas kernels for 0%

commit v1 on v0

--- a/solution.py
+++ b/solution.py
@@ -4,6 +4,11 @@
 from jax.sharding import PartitionSpec as P
 
 exact_prec = lax.Precision.HIGHEST
+
+
+def exchange_gather(shard, axis, dim):
+    sent = jnp.stack([shard] * lax.axis_size(axis))
+    return jnp.concatenate(lax.all_to_all(sent, axis, 0, 0), axis=dim)
 
 
 def mult(left_mat, right_mat):
@@ -15,7 +20,7 @@
     inv_second = diag_inv[section, 1]
     low_block = diag_low[section]
     first_all, second_all, low_all = (
-        lax.all_gather(inv_first, "col", axis=1, tiled=True),
+        exchange_gather(inv_first, "col", 1),
         lax.all_gather(inv_second, "col", axis=1, tiled=True),
         lax.all_gather(low_block, "col", axis=1, tiled=True),
     )

time: 405 us -> 375 us (0.926)
  waiting for transfers between devices: 339 us -> 299 us
  starting transfers between devices: 0.62 us -> 10.6 us
    all_to_all x0 -> x2, waiting for transfers between devices: none -> 49 us  [exchange_gather(): return jnp.concatenate(lax.all_to_all(sent, axis, 0, 0), axis=dim)]
    all_gather x2, waiting for transfers between devices: 45.7 us -> 7.51 us  [inverse_columns(): lax.all_gather(inv_second, 'col', axis=1, tiled=True)]
    all_gather x2 -> x0, waiting for transfers between devices: 36.2 us -> none  [inverse_columns(): lax.all_gather(inv_first, 'col', axis=1, tiled=True)]
    all_gather x2, waiting for transfers between devices: 44.6 us -> 31.4 us  [inverse_columns(): lax.all_gather(low_block, 'col', axis=1, tiled=True)]
    all_to_all x0 -> x2, starting transfers between devices: none -> 10 us  [exchange_gather(): return jnp.concatenate(lax.all_to_all(sent, axis, 0, 0), axis=dim)]
  transfers between devices with their start and end apart: 11 -> 11, of which waited for: 11 -> 10; matrix products, arithmetic and copies ran while one was open for 8% -> 9% of each run, Pallas kernels for 0% -> 0%
where the time goes in v1:
time: 375 us
  waiting for transfers between devices  299 us (80%)
  matrix products  36.8 us (10%)
  between operations  14 us (4%)
  local copies, waits for them, and re-layouts  13.1 us (3%)
  starting transfers between devices  10.6 us (3%)
    psum x2, waiting for transfers between devices, solve_step(): return lax.psum(mult(inverse_cols, rows_block), 'row')  104 us
    all_to_all x2, waiting for transfers between devices, exchange_gather(): return jnp.concatenate(lax.all_to_all(sent, axis, 0, 0), axis=dim)  49 us
    all_gather x1, waiting for transfers between devices, shards(): lax.all_gather(l_trail[1], 'col', axis=1, tiled=True)  47.6 us
    all_gather x1, waiting for transfers between devices, shards(): lax.all_gather(l_trail[0], 'col', axis=1, tiled=True)  37.3 us
    dot_general x9, matrix products, mult(): jnp.dot(left_mat, right_mat, precision=exact_prec, preferred_element_type...  36.8 us
    all_gather x2, waiting for transfers between devices, inverse_columns(): lax.all_gather(low_block, 'col', axis=1, tiled=True)  31.4 us
    all_gather x1, waiting for transfers between devices, shards(): lax.all_gather(l_cross, 'col', axis=1, tiled=True)  20.4 us
    all_to_all x2, starting transfers between devices, exchange_gather(): return jnp.concatenate(lax.all_to_all(sent, axis, 0, 0), axis=dim)  10 us
  transfers between devices with their start and end apart: 11, of which 10 were waited for; matrix products, arithmetic and copies ran while one was open for 9% of the time, Pallas kernels for 0%

profile of v1, /device:TPU:0, one launch (start us, length us, event | category | flops | bytes accessed | tf_op | source)
XLA Modules:
  0.0 374.8 jit_solution(11031896267655203985)
XLA Ops:
  7.2 1.8 fusion.42
  9.1 1.7 fusion.43
  10.9 0.7 all-gather.22.cloned.1.call-update
  12.2 1.1 stack.15
  13.3 6.4 %all-to-all-start = ((f32[8,512,64]{1,2,0:T(8,128)}), f32[8,512,64]{1,2,0:T(8,128)S(1)}, u32[]{:S(2)}, u32[]{:S(2)}) async-start(f32[8,512,64]{1,2,0:T(8,128)} %stack.15), calls=%async_computation | async-start | bytes 2097152 | tf_op jit(solution)/shard_map/all_to_all | solution.py:11
  20.2 34.1 %all-to-all-done = f32[8,512,64]{1,2,0:T(8,128)S(1)} async-done(((f32[8,512,64]{1,2,0:T(8,128)}), f32[8,512,64]{1,2,0:T(8,128)S(1)}, u32[]{:S(2)}, u32[]{:S(2)}) %all-to-all-start) | async-done | bytes 1048608 | tf_op jit(solution)/shard_map/all_to_all | solution.py:11
  54.3 1.1 stack.17
  55.4 3.7 all-to-all-start.1
  59.3 1.1 dynamic-slice_bitcast_fusion.1
  60.4 9.3 %all-gather.16.cloned.1.call-done = f32[1,512,512]{1,2,0:T(8,128)} async-done(((f32[1,512,64]{1,2,0:T(8,128)}), f32[1,512,512]{1,2,0:T(8,128)}) %all-gather.16.cloned.1.call-update) | async-done | bytes 1048592 | tf_op jit(solution)/shard_map/all_gather | solution.py:25
  69.7 2.3 fusion.29
  72.0 2.3 fusion.17
  74.3 2.8 fusion.19
  77.2 14.9 %all-to-all-done.1 = f32[8,512,64]{1,2,0:T(8,128)S(1)} async-done(((f32[8,512,64]{1,2,0:T(8,128)}), f32[8,512,64]{1,2,0:T(8,128)S(1)}, u32[]{:S(2)}, u32[]{:S(2)}) %all-to-all-start.1) | async-done | bytes 1048608 | tf_op jit(solution)/shard_map/all_to_all | solution.py:11
  92.2 7.5 %all-gather.22.cloned.1.call-done = f32[1,1,512,512]{2,3,1,0:T(8,128)} async-done(((f32[1,1,512,64]{2,3,1,0:T(8,128)}), f32[1,1,512,512]{2,3,1,0:T(8,128)}) %all-gather.22.cloned.1.call-update) | async-done | bytes 1048592 | tf_op jit(solution)/shard_map/all_gather | solution.py:24
  99.6 1.1 dynamic-slice_bitcast_fusion
  100.8 22.1 %all-gather.20.cloned.1.call-done = f32[1,512,512]{1,2,0:T(8,128)} async-done(((f32[1,512,64]{1,2,0:T(8,128)}), f32[1,512,512]{1,2,0:T(8,128)}) %all-gather.20.cloned.1.call-update) | async-done | bytes 1048592 | tf_op jit(solution)/shard_map/all_gather | solution.py:25
  122.8 2.3 fusion.26
  125.1 2.3 fusion.16
  127.4 20.4 %all-gather.14.cloned.1.call-done = f32[256,1024]{1,0:T(8,128)} async-done(((f32[256,128]{1,0:T(8,128)}), f32[256,1024]{1,0:T(8,128)}) %all-gather.14.cloned.1.call-update) | async-done | bytes 1048592 | tf_op jit(solution)/shard_map/all_gather | solution.py:47
  147.8 54.7 %all-reduce.5.cloned.1.call-done = f32[1024,256]{1,0:T(8,128)} async-done(((f32[1024,256]{1,0:T(8,128)}), f32[1024,256]{1,0:T(8,128)}) %all-reduce.5.cloned.1.call-update) | async-done | bytes 1048592 | tf_op jit(solution)/shard_map/psum | solution.py:39
  202.5 2.6 fusion.18
  205.2 2.8 fusion.22
  208.0 2.3 fusion.41
  211.5 49.1 %all-reduce.7.cloned.1.call-done = f32[1024,256]{1,0:T(8,128)} async-done(((f32[1024,256]{1,0:T(8,128)}), f32[1024,256]{1,0:T(8,128)}) %all-reduce.7.cloned.1.call-update) | async-done | bytes 1048592 | tf_op jit(solution)/shard_map/psum | solution.py:39
  260.6 1.0 dynamic-slice_bitcast_fusion.2
  261.5 0.8 pad_maximum_fusion
  262.4 47.6 %all-gather.26.cloned.1.call-done = f32[1,1024,1024]{2,1,0:T(8,128)} async-done(((f32[1,1024,128]{2,1,0:T(8,128)}), f32[1,1024,1024]{2,1,0:T(8,128)}) %all-gather.26.cloned.1.call-update) | async-done | bytes 4194320 | tf_op jit(solution)/shard_map/all_gather | solution.py:51
  310.0 10.3 %fusion.13 = f32[1024,256]{0,1:T(8,128)} fusion(f32[1024,256]{1,0:T(8,128)} %all-reduce.7.cloned.1.call-done, f32[1,1024,1024]{2,1,0:T(8,128)} %all-gather.26.cloned.1.call-done), kind=kOutput, calls=%fused_computation.7 | convolution fusion | flops 3221225472 | bytes 6291456 | tf_op jit(solution)/shard_map/dot_general | solution.py:15
  320.3 37.3 %all-gather.24.cloned.1.call-done = f32[1,1024,1024]{2,1,0:T(8,128)} async-done(((f32[1,1024,128]{2,1,0:T(8,128)}), f32[1,1024,1024]{2,1,0:T(8,128)}) %all-gather.24.cloned.1.call-update) | async-done | bytes 4194320 | tf_op jit(solution)/shard_map/all_gather | solution.py:48
  357.6 9.3 %fusion.10 = f32[1024,256]{0,1:T(8,128)S(1)} fusion(f32[1024,256]{0,1:T(8,128)} %fusion.13, f32[1024,256]{0,1:T(8,128)S(1)} %copy.8, f32[1024,256]{1,0:T(8,128)S(1)} %copy-done, f32[1,1024,1024]{2,1,0:T(8,128)} %all-gather.24.cloned.1.call-done), kind=kOutput, calls=%fused_computation.6 | convolution fusion | flops 3221749760 | bytes 8388608 | tf_op jit(solution)/shard_map/dot_general | solution.py:15
  366.9 1.3 copy.9
  (28 shorter events, 2.7 us)
Async XLA Ops:
  7.2 52.1 %all-gather.18.cloned.1.call-start = ((), (), s32[]{:S(2)}) async-start(), calls=%async_computation.6 | async-start | bytes 1179648 | tf_op jit(solution)/shard_map/all_gather | solution.py:24
  9.1 60.7 %all-gather.16.cloned.1.call-start = ((), (), s32[]{:S(2)}) async-start(), calls=%async_computation.5 | async-start | bytes 1179648 | tf_op jit(solution)/shard_map/all_gather | solution.py:25
  10.8 88.8 %all-gather.22.cloned.1.call-start = ((), (), s32[]{:S(2)}) async-start(), calls=%async_computation.8 | async-start | bytes 1179648 | tf_op jit(solution)/shard_map/all_gather | solution.py:24
  11.6 111.3 %all-gather.20.cloned.1.call-start = ((), (), s32[]{:S(2)}) async-start(), calls=%async_computation.7 | async-start | bytes 1179648 | tf_op jit(solution)/shard_map/all_gather | solution.py:25
  13.3 41.0 %all-to-all-start = ((f32[8,512,64]{1,2,0:T(8,128)}), f32[8,512,64]{1,2,0:T(8,128)S(1)}, u32[]{:S(2)}, u32[]{:S(2)}) async-start(f32[8,512,64]{1,2,0:T(8,128)} %stack.15), calls=%async_computation | async-start | bytes 2097152 | tf_op jit(solution)/shard_map/all_to_all | solution.py:11
  19.6 128.2 %all-gather.14.cloned.1.call-start = ((), (), s32[]{:S(2)}) async-start(), calls=%async_computation.3 | async-start | bytes 1179648 | tf_op jit(solution)/shard_map/all_gather | solution.py:47
  55.4 18.9 %copy-start.2 = (f32[2,256,256]{2,1,0:T(8,128)S(1)}, f32[2,256,256]{2,1,0:T(8,128)}, u32[]{:S(2)}) copy-start(f32[2,256,256]{2,1,0:T(8,128)} %param.6) | copy-start | bytes 1572868
  55.4 36.7 %all-to-all-start.1 = ((f32[8,512,64]{1,2,0:T(8,128)}), f32[8,512,64]{1,2,0:T(8,128)S(1)}, u32[]{:S(2)}, u32[]{:S(2)}) async-start(f32[8,512,64]{1,2,0:T(8,128)} %stack.17), calls=%async_computation.1 | async-start | bytes 2097152 | tf_op jit(solution)/shard_map/all_to_all | solution.py:11
  59.1 143.4 %all-reduce.5.cloned.1.call-start = ((), (), s32[]{:S(2)}) async-start(), calls=%async_computation.2 | async-start | bytes 2097152 | tf_op jit(solution)/shard_map/psum | solution.py:39
  77.1 183.4 %all-reduce.7.cloned.1.call-start = ((), (), s32[]{:S(2)}) async-start(), calls=%async_computation.4 | async-start | bytes 2097152 | tf_op jit(solution)/shard_map/psum | solution.py:39
  205.1 6.3 %copy-start = (f32[1024,256]{1,0:T(8,128)S(1)}, f32[1024,256]{1,0:T(8,128)}, u32[]{:S(2)}) copy-start(f32[1024,256]{1,0:T(8,128)} %all-reduce.5.cloned.1.call-done) | copy-start | bytes 3145732
  207.9 3.2 copy-start.1
  208.0 102.0 %all-gather.26.cloned.1.call-start = ((), (), s32[]{:S(2)}) async-start(), calls=%async_computation.10 | async-start | bytes 4718592 | tf_op jit(solution)/shard_map/all_gather | solution.py:51
  210.4 147.3 %all-gather.24.cloned.1.call-start = ((), (), s32[]{:S(2)}) async-start(), calls=%async_computation.9 | async-start | bytes 4718592 | tf_op jit(solution)/shard_map/all_gather | solution.py:48
Sparse Core Ops, SparseCore 0:
  9.6 31.3 all-gather.17
  42.5 27.1 all-gather.15
  71.9 27.6 all-gather.21
  101.1 21.6 all-gather.19
  124.3 23.4 all-gather.13
  151.3 51.1 all-reduce.4
  208.1 52.4 all-reduce.6
  262.1 47.8 all-gather.25
  311.6 45.9 all-gather.23
